TPU v7x, 32 devices: a whole 2x2x4 slice. The times are simulated.
32 devices in a mesh: dp: 4 (over z), expert: 8 (over y, x, core).
Axes of the slice: x: 2, y: 2, z: 4, core: 2. Of those that a mesh axis runs over, the one named last changes fastest.
Arguments:
- layer_input: bfloat16 [16384, 768], P(('dp', 'expert')), may hold values from -6 to 6
- seq_lengths: int32 [32], P(('dp', 'expert')), may hold values from 64 to 512, as said below
- routes: int32 [16384, 2], P(('dp', 'expert')), may hold values from 0 to 9, all different within a row
- ln1_gain: float32 [768], replicated, may hold values from 0.25 to 1.75
- w_query: bfloat16 [768, 768], replicated, may hold values from -0.21875 to 0.21875
- w_key: bfloat16 [768, 768], replicated, may hold values from -0.21875 to 0.21875
- w_value: bfloat16 [768, 768], replicated, may hold values from -0.21875 to 0.21875
- w_output: bfloat16 [768, 768], replicated, may hold values from -0.625 to 0.625
- ln2_gain: float32 [768], replicated, may hold values from 0.25 to 1.75
- w_router: float32 [768, 10], replicated, may hold values from -0.15625 to 0.15625
- frozen_in: bfloat16 [2, 768, 3072], replicated, may hold values from -0.21875 to 0.21875
- frozen_out: bfloat16 [2, 3072, 768], replicated, may hold values from -0.15625 to 0.15625
- new_in: bfloat16 [8, 768, 3072], P('expert'), may hold values from -0.21875 to 0.21875
- new_out: bfloat16 [8, 3072, 768], P('expert'), may hold values from -0.15625 to 0.15625
- cotangent: bfloat16 [16384, 768], P(('dp', 'expert')), may hold values from -6 to 6
Outputs:
- output: float32 [16384, 768], P(('dp', 'expert'))
- grad_input: float32 [16384, 768], P(('dp', 'expert'))
- grad_ln1: float32 [768], replicated
- grad_w_query: float32 [768, 768], replicated
- grad_w_key: float32 [768, 768], replicated
- grad_w_value: float32 [768, 768], replicated
- grad_w_output: float32 [768, 768], replicated
- grad_ln2: float32 [768], replicated
- grad_router: float32 [768, 10], replicated
- grad_new_in: float32 [8, 768, 3072], P('expert', None, 'dp')
- grad_new_out: float32 [8, 3072, 768], P('expert', 'dp')
Inputs may be any that keep to these rules, and one draw needn't show every extreme that they name: `seq_lengths`: in every draw one sequence has exactly 512 valid tokens and another exactly 64. `routes`: the two experts of a token differ.
All inputs are finite; a program needn't handle non-finite values.
Results may differ from a plain program's by a relative error of at most 0.013.
Values may be sent and summed in bfloat16 or wider, within the bound.
A program may use at most 192 MiB of HBM per device.

v0:
```python
import jax
import jax.numpy as jnp
from jax import lax
from jax.sharding import PartitionSpec as P

HEADS = 12
FROZEN = 2
NORM_EPS = 1e-05
GELU_SCALE = 0.7978845608028654
GELU_CUBIC = 0.044715
MASK_VALUE = -1e30


def normalize(values):
    center = values - jnp.mean(values, -1, keepdims=True)
    factor = lax.rsqrt(jnp.mean(center * center, -1, keepdims=True) + NORM_EPS)
    return (center * factor, factor)


def norm_back(grad_normed, normed, factor):
    return factor * (
        grad_normed
        - jnp.mean(grad_normed, -1, keepdims=True)
        - normed * jnp.mean(grad_normed * normed, -1, keepdims=True)
    )


def gelu_value(values):
    return (
        0.5
        * values
        * (1.0 + jnp.tanh(GELU_SCALE * (values + GELU_CUBIC * values * values * values)))
    )


def gelu_slope(values):
    tangent = jnp.tanh(GELU_SCALE * (values + GELU_CUBIC * values * values * values))
    return 0.5 * (1.0 + tangent) + 0.5 * values * (1.0 - tangent * tangent) * GELU_SCALE * (
        1.0 + 3.0 * GELU_CUBIC * values * values
    )


def route_slots(route_rows, length, capacity, new_count):
    tokens = route_rows.shape[0]
    pair_route = jnp.concatenate([route_rows[:, 0], route_rows[:, 1]])
    position = jnp.arange(tokens, dtype=jnp.int32)
    valid = position < length
    pair_valid = jnp.concatenate([valid, valid])
    expert_new = pair_route - FROZEN
    onehot = (
        (expert_new[:, None] == jnp.arange(new_count, dtype=jnp.int32)[None, :])
        & pair_valid[:, None]
    ).astype(jnp.int32)
    before = jnp.cumsum(onehot, 0, dtype=jnp.int32) - onehot
    rank = jnp.sum(before * onehot, 1, dtype=jnp.int32)
    is_new = jnp.sum(onehot, 1, dtype=jnp.int32) > 0
    kept_new = is_new & (rank < capacity)
    slot = jnp.where(kept_new, expert_new * capacity + rank, -1)
    match = slot[None, :] == jnp.arange(new_count * capacity, dtype=jnp.int32)[:, None]
    filled = jnp.any(match, 1)
    slot_pair = jnp.sum(
        jnp.where(match, jnp.arange(2 * tokens, dtype=jnp.int32)[None, :], 0), 1, dtype=jnp.int32
    )
    return (valid, kept_new, slot, filled, slot_pair)


def on_device(
    layer_input,
    seq_lengths,
    routes,
    ln1_gain,
    w_query,
    w_key,
    w_value,
    w_output,
    ln2_gain,
    w_router,
    frozen_in,
    frozen_out,
    new_in,
    new_out,
    cotangent,
):
    tokens, width = layer_input.shape
    head_dim = width // HEADS
    local_new = new_in.shape[0]
    new_count = local_new * lax.axis_size("expert")
    total_experts = FROZEN + new_count
    capacity = 2 * tokens // total_experts
    f32 = jnp.float32
    bf16 = jnp.bfloat16
    scale_value = head_dim ** (-0.5)
    input_rows = layer_input.astype(f32)
    normed_one_f, factor_one = normalize(input_rows)
    normed_one = (normed_one_f * ln1_gain).astype(bf16)
    query_rows = jnp.dot(normed_one, w_query, preferred_element_type=f32).astype(bf16)
    key_rows = jnp.dot(normed_one, w_key, preferred_element_type=f32).astype(bf16)
    value_rows = jnp.dot(normed_one, w_value, preferred_element_type=f32).astype(bf16)
    head_query = query_rows.reshape(tokens, HEADS, head_dim)
    head_key = key_rows.reshape(tokens, HEADS, head_dim)
    head_value = value_rows.reshape(tokens, HEADS, head_dim)
    position = jnp.arange(tokens, dtype=jnp.int32)
    allowed = (position[None, :] <= position[:, None]) & (position[None, :] < seq_lengths[0])

    def masked_scores():
        raw_scores = (
            jnp.einsum("qhd,khd->hqk", head_query, head_key, preferred_element_type=f32)
            * scale_value
        )
        return jnp.where(allowed[None], raw_scores, MASK_VALUE)

    scores = masked_scores()
    peak_value = jnp.max(scores, -1, keepdims=True)
    expo_values = jnp.exp(scores - peak_value)
    row_total = jnp.sum(expo_values, -1, keepdims=True)
    log_total = peak_value + jnp.log(row_total)
    probs_low = (expo_values / row_total).astype(bf16)
    merged = (
        jnp.einsum("hqk,khd->qhd", probs_low, head_value, preferred_element_type=f32)
        .reshape(tokens, width)
        .astype(bf16)
    )
    hidden = input_rows + jnp.dot(merged, w_output, preferred_element_type=f32)
    normed_two_f, factor_two = normalize(hidden)
    normed_two = normed_two_f * ln2_gain
    expert_input = normed_two.astype(bf16)
    logits = jnp.dot(
        normed_two, w_router, precision=lax.Precision.HIGHEST, preferred_element_type=f32
    )
    logit_peak = jnp.max(logits, -1, keepdims=True)
    logit_expo = jnp.exp(logits - logit_peak)
    prob = logit_expo / jnp.sum(logit_expo, -1, keepdims=True)
    route_hot = (
        routes[:, :, None] == jnp.arange(total_experts, dtype=jnp.int32)[None, None, :]
    ).astype(f32)
    chosen = jnp.sum(route_hot * prob[:, None, :], -1)
    chosen_total = jnp.sum(chosen, 1, keepdims=True)
    gates = chosen / chosen_total
    valid, kept_new, slot, filled, slot_pair = route_slots(
        routes, seq_lengths[0], capacity, new_count
    )
    frozen_hot = route_hot[:, :, :FROZEN] * valid.astype(f32)[:, None, None]
    frozen_weight = jnp.sum(frozen_hot * gates[:, :, None], 1)
    frozen_pre = jnp.einsum("td,fde->fte", expert_input, frozen_in, preferred_element_type=f32)
    frozen_act = gelu_value(frozen_pre).astype(bf16)
    frozen_res = jnp.einsum("fte,fed->ftd", frozen_act, frozen_out, preferred_element_type=f32)
    mixture = jnp.sum(frozen_weight.T[:, :, None] * frozen_res, 0)
    slot_token = slot_pair % tokens
    send_rows = jnp.where(filled[:, None], expert_input[slot_token], jnp.zeros((), bf16)).reshape(
        new_count, capacity, width
    )
    received = lax.all_to_all(send_rows, "expert", split_axis=0, concat_axis=1, tiled=True)
    new_pre = jnp.einsum("erd,edf->erf", received, new_in, preferred_element_type=f32)
    new_act = gelu_value(new_pre).astype(bf16)
    new_res = jnp.einsum("erf,efd->erd", new_act, new_out, preferred_element_type=f32).astype(bf16)
    returned = lax.all_to_all(new_res, "expert", split_axis=1, concat_axis=0, tiled=True)
    safe_slot = jnp.maximum(slot, 0)
    pair_res = jnp.where(
        kept_new[:, None], returned.reshape(new_count * capacity, width)[safe_slot].astype(f32), 0.0
    )
    pair_gate = jnp.concatenate([gates[:, 0], gates[:, 1]])
    kept_gate = jnp.where(kept_new, pair_gate, 0.0)
    mixture = (
        mixture
        + kept_gate[:tokens, None] * pair_res[:tokens]
        + kept_gate[tokens:, None] * pair_res[tokens:]
    )
    output = hidden + mixture
    grad_out = cotangent.astype(f32)
    frozen_dot = jnp.einsum("td,ftd->tf", grad_out, frozen_res)
    new_dot = jnp.sum(grad_out[None] * pair_res.reshape(2, tokens, width), -1).T
    grad_gate = jnp.sum(frozen_hot * frozen_dot[:, None, :], -1) + new_dot
    mixing = jnp.sum(grad_gate * gates, 1, keepdims=True)
    grad_chosen = (grad_gate - mixing) / chosen_total
    grad_prob = jnp.sum(route_hot * grad_chosen[:, :, None], 1)
    grad_logits = prob * (grad_prob - jnp.sum(prob * grad_prob, -1, keepdims=True))
    grad_router = jnp.dot(
        normed_two.T, grad_logits, precision=lax.Precision.HIGHEST, preferred_element_type=f32
    )
    frozen_grad_res = (frozen_weight.T[:, :, None] * grad_out[None]).astype(bf16)
    frozen_grad_act = jnp.einsum(
        "ftd,fed->fte", frozen_grad_res, frozen_out, preferred_element_type=f32
    )
    frozen_grad_pre = (frozen_grad_act * gelu_slope(frozen_pre)).astype(bf16)
    grad_expert_in = jnp.einsum(
        "fte,fde->td", frozen_grad_pre, frozen_in, preferred_element_type=f32
    )
    slot_gate = jnp.where(filled, pair_gate[slot_pair], 0.0)
    grad_send = (
        (slot_gate[:, None] * grad_out[slot_token]).astype(bf16).reshape(new_count, capacity, width)
    )
    grad_received = lax.all_to_all(grad_send, "expert", split_axis=0, concat_axis=1, tiled=True)
    new_grad_act = jnp.einsum("erd,efd->erf", grad_received, new_out, preferred_element_type=f32)
    new_grad_pre = (new_grad_act * gelu_slope(new_pre)).astype(bf16)
    grad_sent_rows = jnp.einsum(
        "erf,edf->erd", new_grad_pre, new_in, preferred_element_type=f32
    ).astype(bf16)
    grad_back = lax.all_to_all(grad_sent_rows, "expert", split_axis=1, concat_axis=0, tiled=True)
    back_pair = jnp.where(
        kept_new[:, None],
        grad_back.reshape(new_count * capacity, width)[safe_slot].astype(f32),
        0.0,
    )
    grad_expert_in = grad_expert_in + back_pair[:tokens] + back_pair[tokens:]
    local_in = jnp.einsum("erd,erf->edf", received, new_grad_pre, preferred_element_type=f32)
    local_out = jnp.einsum("erf,erd->efd", new_act, grad_received, preferred_element_type=f32)
    grad_new_in, grad_new_out = (
        lax.psum_scatter(
            local_in.astype(jnp.bfloat16), "dp", scatter_dimension=2, tiled=True
        ).astype(jnp.float32),
        lax.psum_scatter(
            local_out.astype(jnp.bfloat16), "dp", scatter_dimension=1, tiled=True
        ).astype(jnp.float32),
    )
    grad_normed_two = grad_expert_in + jnp.dot(
        grad_logits, w_router.T, precision=lax.Precision.HIGHEST, preferred_element_type=f32
    )
    grad_ln2 = jnp.sum(grad_normed_two * normed_two_f, 0)
    grad_hidden = grad_out + norm_back(grad_normed_two * ln2_gain, normed_two_f, factor_two)
    grad_attn = grad_hidden.astype(bf16)
    grad_w_output = jnp.dot(merged.T, grad_attn, preferred_element_type=f32)
    grad_merged = jnp.dot(grad_attn, w_output.T, preferred_element_type=f32).astype(bf16)
    grad_heads = grad_merged.reshape(tokens, HEADS, head_dim)
    probs_again = jnp.exp(masked_scores() - log_total)
    grad_probs = jnp.einsum("qhd,khd->hqk", grad_heads, head_value, preferred_element_type=f32)
    grad_scores = (
        probs_again * (grad_probs - jnp.sum(probs_again * grad_probs, -1, keepdims=True))
    ).astype(bf16)
    grad_query_rows = (
        (
            jnp.einsum("hqk,khd->qhd", grad_scores, head_key, preferred_element_type=f32)
            * scale_value
        )
        .astype(bf16)
        .reshape(tokens, width)
    )
    grad_key_rows = (
        (
            jnp.einsum("hqk,qhd->khd", grad_scores, head_query, preferred_element_type=f32)
            * scale_value
        )
        .astype(bf16)
        .reshape(tokens, width)
    )
    grad_value_rows = (
        jnp.einsum("hqk,qhd->khd", probs_again.astype(bf16), grad_heads, preferred_element_type=f32)
        .astype(bf16)
        .reshape(tokens, width)
    )
    grad_w_query = jnp.dot(normed_one.T, grad_query_rows, preferred_element_type=f32)
    grad_w_key = jnp.dot(normed_one.T, grad_key_rows, preferred_element_type=f32)
    grad_w_value = jnp.dot(normed_one.T, grad_value_rows, preferred_element_type=f32)
    grad_normed_one = (
        jnp.dot(grad_query_rows, w_query.T, preferred_element_type=f32)
        + jnp.dot(grad_key_rows, w_key.T, preferred_element_type=f32)
        + jnp.dot(grad_value_rows, w_value.T, preferred_element_type=f32)
    )
    grad_ln1 = jnp.sum(grad_normed_one * normed_one_f, 0)
    grad_input = grad_hidden + norm_back(grad_normed_one * ln1_gain, normed_one_f, factor_one)
    summed = lax.psum(
        (grad_ln1, grad_w_query, grad_w_key, grad_w_value, grad_w_output, grad_ln2, grad_router),
        ("dp", "expert"),
    )
    return (
        output,
        grad_input,
        summed[0],
        summed[1],
        summed[2],
        summed[3],
        summed[4],
        summed[5],
        summed[6],
        grad_new_in,
        grad_new_out,
    )


def solution(mesh):
    placed = (
        P(("dp", "expert"), None),
        P(("dp", "expert")),
        P(("dp", "expert"), None),
        P(),
        P(),
        P(),
        P(),
        P(),
        P(),
        P(),
        P(),
        P(),
        P("expert", None, None),
        P("expert", None, None),
        P(("dp", "expert"), None),
    )
    return jax.shard_map(
        on_device,
        mesh=mesh,
        in_specs=placed,
        out_specs=(
            P(("dp", "expert"), None),
            P(("dp", "expert"), None),
            P(),
            P(),
            P(),
            P(),
            P(),
            P(),
            P(),
            P("expert", None, "dp"),
            P("expert", "dp", None),
        ),
        check_vma=False,
    )
```

profile of v0, /device:TPU:0, one launch (start us, length us, event | category | flops | bytes accessed | tf_op | source)
XLA Modules:
  0.0 569.3 jit_solution(2203841953963201932)
XLA Ops:
  33.2 3.8 fusion.7
  50.4 4.0 gather_fusion
  57.2 5.2 all-to-all-start
  64.2 5.8 %gather_fusion.2 = f32[816]{0:T(1024)} fusion(f32[1024]{0:T(1024)S(1)} %get-tuple-element.39, s32[1024]{0:T(1024)} %pad_clamp_fusion), kind=kCustom, calls=%fused_computation.2 | custom fusion | bytes 9792 | tf_op jit(solution)/shard_map/gather | solution.py:188
  71.4 4.0 gather_fusion.3
  82.1 4.3 all-to-all-start.2
  89.1 10.5 %fusion.26 = f32[816,3072]{1,0:T(8,128)} fusion(bf16[816,768]{1,0:T(8,128)(2,1)} %reshape.485, bf16[1,768,3072]{2,1,0:T(8,128)(2,1)} %param.27), kind=kOutput, calls=%fused_computation.45 | convolution fusion | flops 3850371072 | bytes 15998976 | tf_op jit(solution)/shard_map/erd,edf->erf/dot_general | solution.py:153
  99.7 4.6 all-to-all-done.2
  106.5 11.4 %fusion.29 = bf16[1,3072,768]{2,1,0:T(8,128)(2,1)} fusion(bf16[816,768]{1,0:T(8,128)(2,1)} %reshape.489, f32[816,3072]{1,0:T(8,128)} %fusion.26), kind=kOutput, calls=%fused_computation.48 | convolution fusion | flops 3875291136 | bytes 15998976 | tf_op jit(solution)/shard_map/erf,erd->efd/dot_general | solution.py:206
  118.0 7.6 %fusion.79 = f32[512,2,3072]{2,0,1:T(8,128)S(1)} fusion(bf16[2,768,3072]{2,1,0:T(8,128)(2,1)} %param.25, bf16[512,768]{1,0:T(8,128)(2,1)S(1)} %multiply_convert_fusion.12), kind=kOutput, calls=%fused_computation.120 | convolution fusion | flops 4831838208 | bytes 22806528 | tf_op jit(solution)/shard_map/td,fde->fte/dot_general | solution.py:144
  125.6 13.5 %fusion.19 = f32[2,512,768]{2,1,0:T(8,128)S(1)} fusion(bf16[2,3072,768]{2,1,0:T(8,128)(2,1)} %param.26, f32[512,2,3072]{2,0,1:T(8,128)S(1)} %fusion.79), kind=kOutput, calls=%fused_computation.36 | convolution fusion | flops 4860149760 | bytes 25165824 | tf_op jit(solution)/shard_map/fte,fed->ftd/dot_general | solution.py:146
  140.8 6.2 %fusion.34 = f32[512,1,2]{2,1,0:T(1,128)} fusion(f32[2,512,768]{2,1,0:T(8,128)S(1)} %fusion.19, bf16[512,768,1]{1,0,2:T(8,128)(2,1)S(1)} %bitcast.168), kind=kOutput, calls=%fused_computation.60 | convolution fusion | flops 1572864 | bytes 3936256 | tf_op jit(solution)/shard_map/td,ftd->tf/dot_general | solution.py:170
  157.5 9.9 %fusion.64 = bf16[1,816,768]{2,1,0:T(8,128)(2,1)S(1)} fusion(bf16[1,3072,768]{2,1,0:T(8,128)(2,1)} %param.28, f32[816,3072]{1,0:T(8,128)} %fusion.26), kind=kOutput, calls=%fused_computation.100 | convolution fusion | flops 3873558528 | bytes 15998976 | tf_op jit(solution)/shard_map/erf,efd->erd/dot_general | solution.py:155
  171.3 10.3 %reduce.10 = bf16[816,768]{1,0:T(8,128)(2,1)} reduce(bf16[816,1,768]{2,1,0:T(2,128)(2,1)} %bitcast.160, bf16[]{:T(256)} %broadcast.531), dimensions={1}, to_apply=%bitcast.148.reduce_sub_computation | reduce | bytes 2506754
  183.9 4.3 all-to-all-start.1
  188.2 12.6 %fusion.14 = bf16[816,3072]{1,0:T(8,128)(2,1)S(1)} fusion(f32[816,3072]{1,0:T(8,128)} %fusion.26, bf16[816,768]{1,0:T(8,128)(2,1)} %reshape.489, bf16[1,3072,768]{2,1,0:T(8,128)(2,1)} %param.28), kind=kOutput, calls=%fused_computation.31 | convolution fusion | flops 3897999360 | bytes 21012480 | tf_op jit(solution)/shard_map/erd,efd->erf/dot_general | solution.py:193
  200.8 8.2 %fusion.67 = bf16[1,816,768]{2,1,0:T(8,128)(2,1)S(1)} fusion(bf16[816,3072]{1,0:T(8,128)(2,1)S(1)} %fusion.14, bf16[1,768,3072]{2,1,0:T(8,128)(2,1)} %param.27), kind=kOutput, calls=%fused_computation.101 | convolution fusion | flops 3850997760 | bytes 10985472 | tf_op jit(solution)/shard_map/erf,edf->erd/dot_general | solution.py:195
  212.4 10.5 %reduce.11 = bf16[816,768]{1,0:T(8,128)(2,1)} reduce(bf16[816,1,768]{2,1,0:T(2,128)(2,1)} %bitcast.161, bf16[]{:T(256)} %broadcast.531), dimensions={1}, to_apply=%bitcast.147.reduce_sub_computation | reduce | bytes 2506754
  225.1 4.3 all-to-all-start.3
  230.2 8.8 %fusion.28 = bf16[1,768,3072]{2,1,0:T(8,128)(2,1)} fusion(bf16[816,768]{1,0:T(8,128)(2,1)} %reshape.485, bf16[816,3072]{1,0:T(8,128)(2,1)} %copy-done.66), kind=kOutput, calls=%fused_computation.47 | convolution fusion | flops 3852730368 | bytes 10985472 | tf_op jit(solution)/shard_map/erd,erf->edf/dot_general | solution.py:205
  239.0 6.5 %reshape.543 = bf16[816,1,768]{2,1,0:T(2,128)(2,1)} reshape(bf16[8,2,39168]{2,1,0:T(2,128)(2,1)} %all-to-all-done.1) | data formatting | bytes 2506752
  248.6 6.5 %reshape.545 = bf16[816,1,768]{2,1,0:T(2,128)(2,1)} reshape(bf16[8,2,39168]{2,1,0:T(2,128)(2,1)} %all-to-all-done.3) | data formatting | bytes 2506752
  258.1 7.0 %gather_fusion.1 = bf16[1024,768]{1,0:T(8,128)(2,1)} fusion(bf16[816,768]{1,0:T(8,128)(2,1)} %bitcast.154, s32[1024]{0:T(1024)S(1)} %broadcast_clamp_fusion), kind=kCustom, calls=%fused_computation.1 | custom fusion | bytes 3149824 | tf_op jit(solution)/shard_map/gather | solution.py:159
  265.1 7.0 %gather_fusion.4 = bf16[1024,768]{1,0:T(8,128)(2,1)} fusion(bf16[816,768]{1,0:T(8,128)(2,1)} %bitcast.155, s32[1024]{0:T(1024)S(1)} %broadcast_clamp_fusion), kind=kCustom, calls=%fused_computation.4 | custom fusion | bytes 3149824 | tf_op jit(solution)/shard_map/gather | solution.py:201
  272.2 5.9 %fusion.33 = (f32[1024]{0:T(1024)}, f32[1024,768]{1,0:T(8,128)}, f32[1024,768]{1,0:T(8,128)}) fusion(f32[512,768]{1,0:T(8,128)S(1)} %convert_element_type.157, bf16[1024,768]{1,0:T(8,128)(2,1)} %gather_fusion.1, pred[1024]{0:T(1024)(128)(4,1)} %copy-done.61, bf16[1024,768]{1,0:T(8,128)(2,1)} %gather_fusion.4), kind=kLoop, calls=%fused_computation.55 | loop fusion | flops 4717568 | bytes 11015168 | tf_op jit(solution)/shard_map/reduce_sum | solution.py:171
  285.1 21.6 %multiply_reduce_fusion.2 = (f32[768]{0:T(1024)}, f32[512]{0:T(512)}, f32[512]{0:T(512)}, f32[512,768]{1,0:T(8,128)}) fusion(f32[512]{0:T(512)S(1)} %copy-done.41, f32[512,768]{1,0:T(8,128)} %copy-done.2, f32[512]{0:T(512)S(1)} %broadcast_multiply_fusion.4, f32[768]{0:T(1024)S(1)} %copy-done.37, f32[512,768]{1,0:T(8,128)} %fusion.93, ...), kind=kOutput, calls=%fused_computation.89 | convolution fusion | flops 9729341440 | bytes 40912896 | tf_op jit(solution)/shard_map/fte,fde->td/dot_general | solution.py:185
  308.2 4.9 multiply_add_fusion.2
  315.1 8.0 %fusion.70 = bf16[12,64,512]{2,1,0:T(8,128)(2,1)S(1)} fusion(bf16[512,12,64]{0,2,1:T(8,128)(2,1)} %bitcast.166, f32[12,512]{1,0:T(8,128)} %log_add_fusion, f32[12,512,512]{1,2,0:T(8,128)} %copy-done.1, pred[512,512]{0,1:T(8,128)(4,1)} %fusion.78), kind=kOutput, calls=%fused_computation.106 | convolution fusion | flops 415629312 | bytes 14442496 | tf_op jit(solution)/shard_map/hqk,qhd->khd/dot_general | solution.py:246
  326.5 10.2 %multiply_reduce_fusion = (f32[12,512]{1,0:T(8,128)S(1)}, f32[12,512,512]{1,2,0:T(8,128)}) fusion(f32[12,512]{1,0:T(8,128)S(1)} %copy-done.33, f32[12,512,512]{1,2,0:T(8,128)} %copy-done.1, pred[512,512]{0,1:T(8,128)(4,1)S(1)} %copy-done.13, bf16[512,12,64]{0,2,1:T(8,128)(2,1)S(1)} %bitcast.167, bf16[512,12,64]{0,2,1:T(8,128)(2,1)S(1)} %bitcast.165), kind=kOutput, calls=%fused_computation.18 | convolution fusion | flops 418375680 | bytes 27049984 | tf_op jit(solution)/shard_map/qhd,khd->hqk/dot_general | solution.py:225
  336.8 7.3 %multiply_convert_fusion = bf16[12,512,512]{1,2,0:T(8,128)(2,1)S(1)} fusion(f32[12,512,512]{1,2,0:T(8,128)} %get-tuple-element.55, f32[12,512]{1,0:T(8,128)S(1)} %get-tuple-element.54, f32[12,512]{1,0:T(8,128)S(1)} %copy-done.33, f32[12,512,512]{1,2,0:T(8,128)S(1)} %bitcast.153, pred[512,512]{0,1:T(8,128)(4,1)S(1)} %copy-done.13), kind=kLoop, calls=%fused_computation.17 | loop fusion | flops 18874368 | bytes 31768576 | tf_op jit(solution)/shard_map/convert_element_type | solution.py:228
  366.8 45.1 %all-reduce = (f32[768]{0:T(1024)}, f32[768]{0:T(1024)}, f32[768,10]{0,1:T(8,128)}) all-reduce(f32[768]{0:T(1024)S(1)} %get-tuple-element.13, f32[768]{0:T(1024)} %get-tuple-element.11, f32[768,10]{0,1:T(8,128)} %fusion.74), channel_id=1, replica_groups=mesh['dp'=4,'expert'=8] {'dp','expert'}, use_global_device_ids=true, to_apply=%region_29.30 | all-reduce | flops 9216 | bytes 73728 | tf_op jit(solution)/shard_map/psum | solution.py:260
  422.1 129.5 %all-reduce.4.cloned.1.call-done = (f32[768,768]{1,0:T(8,128)}, f32[768,768]{1,0:T(8,128)}, f32[768,768]{1,0:T(8,128)}, f32[768,768]{1,0:T(8,128)}) async-done(((f32[768,768]{1,0:T(8,128)}, f32[768,768]{1,0:T(8,128)}, f32[768,768]{1,0:T(8,128)}, f32[768,768]{1,0:T(8,128)}), (f32[768,768]{1,0:T(8,128)}, f32[768,768]{1,0:T(8,128)}, f32[768,768]{1,0:T(8,128)}, ...) | async-done | bytes 9437200 | tf_op jit(solution)/shard_map/psum | solution.py:260
  (252 shorter events, 142.1 us)
Async XLA Ops:
  8.0 17.4 %copy-start = (bf16[768,768]{1,0:T(8,128)(2,1)S(1)}, bf16[768,768]{1,0:T(8,128)(2,1)}, u32[]{:S(2)}) copy-start(bf16[768,768]{1,0:T(8,128)(2,1)} %param.21) | copy-start | bytes 3538948
  12.1 13.2 %copy-start.47 = (f32[512]{0:T(512)}, f32[512]{0:T(512)S(1)}, u32[]{:S(2)}) copy-start(f32[512]{0:T(512)S(1)} %broadcast_multiply_fusion.5) | copy-start | bytes 6148
  13.6 11.7 %copy-start.52 = (f32[512]{0:T(512)}, f32[512]{0:T(512)S(1)}, u32[]{:S(2)}) copy-start(f32[512]{0:T(512)S(1)} %add_rsqrt_fusion.1) | copy-start | bytes 6148
  14.4 31.7 %copy-start.42 = (s32[512,1]{0,1:T(1,128)}, s32[512,1]{0,1:T(1,128)S(1)}, u32[]{:S(2)}) copy-start(s32[512,1]{0,1:T(1,128)S(1)} %get-tuple-element.42) | copy-start | bytes 6148
  14.4 31.7 %copy-start.43 = (s32[512,1]{0,1:T(1,128)}, s32[512,1]{0,1:T(1,128)S(1)}, u32[]{:S(2)}) copy-start(s32[512,1]{0,1:T(1,128)S(1)} %get-tuple-element.43) | copy-start | bytes 6148
  20.6 9.5 %copy-start.8 = (bf16[512,768]{0,1:T(8,128)(2,1)}, bf16[512,768]{0,1:T(8,128)(2,1)S(1)}, u32[]{:S(2)}) copy-start(bf16[512,768]{0,1:T(8,128)(2,1)S(1)} %copy.82) | copy-start | bytes 2359300
  42.7 6.2 %copy-start.2 = (f32[512,768]{1,0:T(8,128)}, f32[512,768]{1,0:T(8,128)S(1)}, u32[]{:S(2)}) copy-start(f32[512,768]{1,0:T(8,128)S(1)} %get-tuple-element.50) | copy-start | bytes 4718596
  43.1 5.8 %copy-start.40 = (f32[512]{0:T(512)}, f32[512]{0:T(512)S(1)}, u32[]{:S(2)}) copy-start(f32[512]{0:T(512)S(1)} %add_rsqrt_fusion) | copy-start | bytes 6148
  49.2 6.7 %copy-start.60 = (pred[8,102]{1,0:T(8,128)(4,1)}, pred[8,102]{1,0:T(8,128)(4,1)S(1)}, u32[]{:S(2)}) copy-start(pred[8,102]{1,0:T(8,128)(4,1)S(1)} %broadcast_in_dim.76) | copy-start | bytes 2452
  57.2 24.9 %all-to-all-start = ((bf16[8,102,768]{2,1,0:T(8,128)(2,1)}), bf16[8,102,768]{2,1,0:T(8,128)(2,1)}, u32[]{:S(2)}, u32[]{:S(2)}) async-start(bf16[8,102,768]{2,1,0:T(8,128)(2,1)} %broadcast_select_fusion), calls=%async_computation | async-start | bytes 2555904 | tf_op jit(solution)/shard_map/all_to_all | solution.py:152
  82.1 22.2 %all-to-all-start.2 = ((bf16[8,102,768]{2,1,0:T(8,128)(2,1)}), bf16[8,102,768]{2,1,0:T(8,128)(2,1)}, u32[]{:S(2)}, u32[]{:S(2)}) async-start(bf16[8,102,768]{2,1,0:T(8,128)(2,1)} %multiply_convert_fusion.5), calls=%async_computation.2 | async-start | bytes 2555904 | tf_op jit(solution)/shard_map/all_to_all | solution.py:192
  86.3 330.0 %reduce-scatter.5.cloned.1.call-start = ((), (), s32[]{:S(2)}) async-start(), calls=%async_computation.7 | async-start | bytes 5898240 | tf_op jit(solution)/shard_map/reduce_scatter | solution.py:211
  125.6 13.5 %copy-start.67 = (f32[512,2,3072]{2,0,1:T(8,128)}, f32[512,2,3072]{2,0,1:T(8,128)S(1)}, u32[]{:S(2)}) copy-start(f32[512,2,3072]{2,0,1:T(8,128)S(1)} %fusion.79) | copy-start | bytes 37748740
  125.6 15.2 %copy-start.17 = (bf16[512,768]{1,0:T(8,128)(2,1)S(1)}, bf16[512,768]{1,0:T(8,128)(2,1)}, u32[]{:S(2)}) copy-start(bf16[512,768]{1,0:T(8,128)(2,1)} %param.29) | copy-start | bytes 2359300
  140.8 7.9 %copy-start.39 = (s32[512,2]{0,1:T(2,128)S(1)}, s32[512,2]{0,1:T(2,128)}, u32[]{:S(2)}) copy-start(s32[512,2]{0,1:T(2,128)} %param.17) | copy-start | bytes 12292
  183.9 41.2 %all-to-all-start.1 = ((bf16[8,2,39168]{2,1,0:T(2,128)(2,1)}), bf16[8,2,39168]{2,1,0:T(2,128)(2,1)}, u32[]{:S(2)}, u32[]{:S(2)}) async-start(bf16[8,2,39168]{2,1,0:T(2,128)(2,1)} %reshape.542), calls=%async_computation.1 | async-start | bytes 2506752 | tf_op jit(solution)/shard_map/all_to_all | solution.py:156
  200.8 8.3 %copy-start.66 = (bf16[816,3072]{1,0:T(8,128)(2,1)}, bf16[816,3072]{1,0:T(8,128)(2,1)S(1)}, u32[]{:S(2)}) copy-start(bf16[816,3072]{1,0:T(8,128)(2,1)S(1)} %fusion.14) | copy-start | bytes 15040516
  225.1 23.5 %all-to-all-start.3 = ((bf16[8,2,39168]{2,1,0:T(2,128)(2,1)}), bf16[8,2,39168]{2,1,0:T(2,128)(2,1)}, u32[]{:S(2)}, u32[]{:S(2)}) async-start(bf16[8,2,39168]{2,1,0:T(2,128)(2,1)} %reshape.544), calls=%async_computation.3 | async-start | bytes 2506752 | tf_op jit(solution)/shard_map/all_to_all | solution.py:198
  229.4 189.8 %reduce-scatter.3.cloned.1.call-start = ((), (), s32[]{:S(2)}) async-start(), calls=%async_computation.6 | async-start | bytes 5898240 | tf_op jit(solution)/shard_map/reduce_scatter | solution.py:208
  239.0 312.6 %all-reduce.4.cloned.1.call-start = ((), (), s32[]{:S(2)}) async-start(), calls=%async_computation.8 | async-start | bytes 18874368 | tf_op jit(solution)/shard_map/psum | solution.py:260
  272.2 13.0 %copy-start.41 = (f32[512]{0:T(512)S(1)}, f32[512]{0:T(512)}, u32[]{:S(2)}) copy-start(f32[512]{0:T(512)} %copy-done.40) | copy-start | bytes 6148
  281.7 25.1 %copy-start.51 = (f32[512]{0:T(512)}, f32[512]{0:T(512)S(1)}, u32[]{:S(2)}) copy-start(f32[512]{0:T(512)S(1)} %multiply_reduce_fusion.7) | copy-start | bytes 6148
  313.1 40.8 %copy-start.4 = (f32[512,768]{1,0:T(8,128)}, f32[512,768]{1,0:T(8,128)S(1)}, u32[]{:S(2)}) copy-start(f32[512,768]{1,0:T(8,128)S(1)} %get-tuple-element.37) | copy-start | bytes 4718596
  315.1 9.0 %copy-start.7 = (bf16[512,768]{1,0:T(8,128)(2,1)S(1)}, bf16[512,768]{1,0:T(8,128)(2,1)}, u32[]{:S(2)}) copy-start(bf16[512,768]{1,0:T(8,128)(2,1)} %param.15) | copy-start | bytes 2359300
  315.1 9.0 %copy-start.48 = (f32[512]{0:T(512)S(1)}, f32[512]{0:T(512)}, u32[]{:S(2)}) copy-start(f32[512]{0:T(512)} %copy-done.47) | copy-start | bytes 6148
  315.1 9.0 %copy-start.53 = (f32[512]{0:T(512)S(1)}, f32[512]{0:T(512)}, u32[]{:S(2)}) copy-start(f32[512]{0:T(512)} %copy-done.52) | copy-start | bytes 6148
  315.1 9.0 %copy-start.56 = (f32[768]{0:T(1024)S(1)}, f32[768]{0:T(1024)}, u32[]{:S(2)}) copy-start(f32[768]{0:T(1024)} %param.18) | copy-start | bytes 9220
  324.1 12.7 %slice-start = ((s8[12582912]{0:T(1024)(128)(4,1)}), s8[4194304]{0:T(1024)(128)(4,1)S(1)}, s32[]{:S(2)}) async-start(s8[12582912]{0:T(1024)(128)(4,1)} %bitcast.152), calls=%async_computation.9 | async-start | bytes 8388608
  326.5 10.2 %slice-start.1 = ((s8[12582912]{0:T(1024)(128)(4,1)}), s8[4194304]{0:T(1024)(128)(4,1)S(1)}, s32[]{:S(2)}) async-start(s8[12582912]{0:T(1024)(128)(4,1)} %bitcast.152), calls=%async_computation.10 | async-start | bytes 8388608
  326.5 10.2 %slice-start.2 = ((s8[12582912]{0:T(1024)(128)(4,1)}), s8[4194304]{0:T(1024)(128)(4,1)S(1)}, s32[]{:S(2)}) async-start(s8[12582912]{0:T(1024)(128)(4,1)} %bitcast.152), calls=%async_computation.11 | async-start | bytes 8388608
  336.7 7.3 %copy-start.11 = (bf16[512,768]{0,1:T(8,128)(2,1)S(1)}, bf16[512,768]{0,1:T(8,128)(2,1)}, u32[]{:S(2)}) copy-start(bf16[512,768]{0,1:T(8,128)(2,1)} %copy-done.10) | copy-start | bytes 2359300
  363.7 49.6 %copy-start.5 = (f32[512,768]{1,0:T(8,128)S(1)}, f32[512,768]{1,0:T(8,128)}, u32[]{:S(2)}) copy-start(f32[512,768]{1,0:T(8,128)} %copy-done.4) | copy-start | bytes 4718596
  (46 other events, 122.1 us)
Sparse Core Ops, SparseCore 0:
  118.1 85.1 reduce-scatter.4
  239.1 87.3 reduce-scatter.2
Sparse Core Ops, SparseCore 1:
  356.2 195.3 all-reduce.3
where the time goes:
time: 579 us; the launch traced here: 569 us
  matrix products  172 us (30%)
  waiting for transfers between devices  134 us (23%)
  local copies, waits for them, and re-layouts  99.2 us (17%)
  other arithmetic  83.1 us (14%)
  blocking collectives  45.1 us (8%)
  starting transfers between devices  18.1 us (3%)
  between operations  17.6 us (3%)
    psum x1, waiting for transfers between devices, on_device(): lax.psum((grad_ln1, grad_w_query, grad_w_key, grad_w_value, grad_w_output...  129 us
    psum x1, blocking collectives, on_device(): lax.psum((grad_ln1, grad_w_query, grad_w_key, grad_w_value, grad_w_output...  45.1 us
    unnamed x153, local copies, waits for them, and re-layouts  43.1 us
    dot_general x1, matrix products, on_device(): jnp.einsum('fte,fde->td', frozen_grad_pre, frozen_in, preferred_element_t...  21.6 us
    unnamed x4, other arithmetic  21.5 us
    dot_general x1, matrix products, on_device(): jnp.einsum('fte,fed->ftd', frozen_act, frozen_out, preferred_element_type...  13.5 us
    dot_general x1, matrix products, on_device(): jnp.einsum('erd,efd->erf', grad_received, new_out, preferred_element_type...  12.6 us
  transfers between devices with their start and end apart: 7, of which 2 were waited for; matrix products, arithmetic and copies ran while one was open for 49% of the time, Pallas kernels for 0%

commit v1 on v0

--- a/solution.py
+++ b/solution.py
@@ -257,10 +257,17 @@
     )
     grad_ln1 = jnp.sum(grad_normed_one * normed_one_f, 0)
     grad_input = grad_hidden + norm_back(grad_normed_one * ln1_gain, normed_one_f, factor_one)
-    summed = lax.psum(
-        (grad_ln1, grad_w_query, grad_w_key, grad_w_value, grad_w_output, grad_ln2, grad_router),
-        ("dp", "expert"),
-    )
+    summed = (
+        grad_ln1,
+        grad_w_query,
+        grad_w_key,
+        grad_w_value,
+        grad_w_output,
+        grad_ln2,
+        grad_router,
+    )
+    for axis in ("expert", "dp"):
+        summed = lax.psum(summed, axis)
     return (
         output,
         grad_input,

time: 579 us -> 878 us (1.52)
  waiting for transfers between devices: 134 us -> 429 us
    psum x1 -> x2, waiting for transfers between devices: 129 us -> 428 us  [on_device(): summed = lax.psum(summed, axis)]
    psum x1 -> x2, blocking collectives: 45.1 us -> 46.6 us  [on_device(): summed = lax.psum(summed, axis)]
    unnamed x153 -> x155, local copies, waits for them, and re-layouts: 43.1 us -> 42.3 us
  transfers between devices with their start and end apart: 7 -> 8, of which waited for: 2 -> 3; matrix products, arithmetic and copies ran while one was open for 49% -> 22% of each run, Pallas kernels for 0% -> 0%
where the time goes in v1:
time: 878 us; the launch traced here: 868 us
  waiting for transfers between devices  429 us (49%)
  matrix products  177 us (20%)
  local copies, waits for them, and re-layouts  98 us (11%)
  other arithmetic  81.8 us (9%)
  blocking collectives  46.6 us (5%)
  starting transfers between devices  18.2 us (2%)
  between operations  17.8 us (2%)
    psum x2, waiting for transfers between devices, on_device(): summed = lax.psum(summed, axis)  428 us
    psum x2, blocking collectives, on_device(): summed = lax.psum(summed, axis)  46.6 us
    unnamed x155, local copies, waits for them, and re-layouts  42.3 us
    unnamed x4, other arithmetic  21.9 us
    dot_general x1, matrix products, on_device(): jnp.einsum('fte,fde->td', frozen_grad_pre, frozen_in, preferred_element_t...  21.5 us
  transfers between devices with their start and end apart: 8, of which 3 were waited for; matrix products, arithmetic and copies ran while one was open for 22% of the time, Pallas kernels for 0%

profile of v1, /device:TPU:0, one launch (start us, length us, event | category | flops | bytes accessed | tf_op | source)
XLA Modules:
  0.0 868.0 jit_solution(11732499905417853261)
XLA Ops:
  49.8 4.0 gather_fusion
  58.6 5.2 all-to-all-start
  63.8 7.6 fusion.79
  71.4 13.5 %fusion.19 = f32[2,512,768]{2,1,0:T(8,128)S(1)} fusion(bf16[2,3072,768]{2,1,0:T(8,128)(2,1)} %param.26, f32[512,2,3072]{2,0,1:T(8,128)S(1)} %fusion.79), kind=kOutput, calls=%fused_computation.36 | convolution fusion | flops 4860149760 | bytes 25165824 | tf_op jit(solution)/shard_map/fte,fed->ftd/dot_general | solution.py:146
  85.0 6.1 fusion.34
  92.3 5.8 gather_fusion.2
  99.5 4.1 gather_fusion.3
  113.3 4.3 all-to-all-start.2
  119.8 15.0 %fusion.26 = f32[816,3072]{1,0:T(8,128)S(1)} fusion(bf16[816,768]{1,0:T(8,128)(2,1)} %reshape.485, bf16[1,768,3072]{2,1,0:T(8,128)(2,1)} %param.27), kind=kOutput, calls=%fused_computation.45 | convolution fusion | flops 3850371072 | bytes 15998976 | tf_op jit(solution)/shard_map/erd,edf->erf/dot_general | solution.py:153
  134.9 11.8 %fusion.64 = bf16[1,816,768]{2,1,0:T(8,128)(2,1)S(1)} fusion(bf16[1,3072,768]{2,1,0:T(8,128)(2,1)} %param.28, f32[816,3072]{1,0:T(8,128)S(1)} %fusion.26), kind=kOutput, calls=%fused_computation.100 | convolution fusion | flops 3873558528 | bytes 15998976 | tf_op jit(solution)/shard_map/erf,efd->erd/dot_general | solution.py:155
  150.6 10.7 %reduce.10 = bf16[816,768]{1,0:T(8,128)(2,1)} reduce(bf16[816,1,768]{2,1,0:T(2,128)(2,1)} %bitcast.160, bf16[]{:T(256)} %broadcast.531), dimensions={1}, to_apply=%bitcast.148.reduce_sub_computation | reduce | bytes 2506754
  163.5 4.3 all-to-all-start.1
  170.1 12.1 %fusion.14 = bf16[816,3072]{1,0:T(8,128)(2,1)S(1)} fusion(f32[816,3072]{1,0:T(8,128)} %copy-done.68, bf16[816,768]{1,0:T(8,128)(2,1)} %reshape.489, bf16[1,3072,768]{2,1,0:T(8,128)(2,1)} %param.28), kind=kOutput, calls=%fused_computation.31 | convolution fusion | flops 3897999360 | bytes 21012480 | tf_op jit(solution)/shard_map/erd,efd->erf/dot_general | solution.py:193
  182.2 8.2 fusion.67
  193.8 10.5 %reduce.11 = bf16[816,768]{1,0:T(8,128)(2,1)} reduce(bf16[816,1,768]{2,1,0:T(2,128)(2,1)} %bitcast.161, bf16[]{:T(256)} %broadcast.531), dimensions={1}, to_apply=%bitcast.147.reduce_sub_computation | reduce | bytes 2506754
  206.6 4.3 all-to-all-start.3
  217.8 6.5 reshape.543
  228.5 6.5 reshape.545
  237.9 7.0 gather_fusion.1
  244.9 7.0 gather_fusion.4
  252.0 5.9 fusion.33
  264.8 21.5 %multiply_reduce_fusion.2 = (f32[768]{0:T(1024)}, f32[512]{0:T(512)}, f32[512]{0:T(512)}, f32[512,768]{1,0:T(8,128)}) fusion(f32[512]{0:T(512)S(1)} %copy-done.42, f32[512,768]{1,0:T(8,128)} %copy-done.2, f32[512]{0:T(512)S(1)} %broadcast_multiply_fusion.4, f32[768]{0:T(1024)S(1)} %copy-done.38, f32[512,768]{1,0:T(8,128)} %fusion.93, ...), kind=kOutput, calls=%fused_computation.89 | convolution fusion | flops 9729341440 | bytes 40912896 | tf_op jit(solution)/shard_map/fte,fde->td/dot_general | solution.py:185
  287.7 4.7 multiply_add_fusion.2
  296.7 7.5 fusion.70
  304.2 9.5 %multiply_reduce_fusion = (f32[12,512]{1,0:T(8,128)S(1)}, f32[12,512,512]{1,2,0:T(8,128)}) fusion(f32[12,512]{1,0:T(8,128)S(1)} %copy-done.34, f32[12,512,512]{1,2,0:T(8,128)} %copy-done.1, pred[512,512]{0,1:T(8,128)(4,1)S(1)} %copy-done.13, bf16[512,12,64]{0,2,1:T(8,128)(2,1)S(1)} %bitcast.167, bf16[512,12,64]{0,2,1:T(8,128)(2,1)S(1)} %bitcast.165), kind=kOutput, calls=%fused_computation.18 | convolution fusion | flops 418375680 | bytes 27049984 | tf_op jit(solution)/shard_map/qhd,khd->hqk/dot_general | solution.py:225
  313.8 7.1 multiply_convert_fusion
  333.2 11.2 %fusion.29 = bf16[1,3072,768]{2,1,0:T(8,128)(2,1)} fusion(bf16[816,768]{1,0:T(8,128)(2,1)S(1)} %copy-done.24, f32[816,3072]{1,0:T(8,128)} %copy-done.68), kind=kOutput, calls=%fused_computation.48 | convolution fusion | flops 3875291136 | bytes 15998976 | tf_op jit(solution)/shard_map/erf,erd->efd/dot_general | solution.py:206
  345.7 9.3 %fusion.28 = bf16[1,768,3072]{2,1,0:T(8,128)(2,1)} fusion(bf16[816,768]{1,0:T(8,128)(2,1)S(1)} %copy-done.23, bf16[816,3072]{1,0:T(8,128)(2,1)} %copy-done.66), kind=kOutput, calls=%fused_computation.47 | convolution fusion | flops 3852730368 | bytes 10985472 | tf_op jit(solution)/shard_map/erd,erf->edf/dot_general | solution.py:205
  355.1 116.9 %all-reduce.7.cloned.1.call-done = (f32[768,768]{1,0:T(8,128)}, f32[768,768]{1,0:T(8,128)}, f32[768,768]{1,0:T(8,128)}, f32[768,768]{1,0:T(8,128)}) async-done(((f32[768,768]{1,0:T(8,128)}, f32[768,768]{1,0:T(8,128)}, f32[768,768]{1,0:T(8,128)}, f32[768,768]{1,0:T(8,128)}), (f32[768,768]{1,0:T(8,128)}, f32[768,768]{1,0:T(8,128)}, f32[768,768]{1,0:T(8,128)}, ...) | async-done | bytes 9437200 | tf_op jit(solution)/shard_map/psum | solution.py:270
  482.7 25.0 %all-reduce = (f32[768]{0:T(1024)}, f32[768]{0:T(1024)}, f32[768,10]{0,1:T(8,128)}) all-reduce(f32[768]{0:T(1024)S(1)} %get-tuple-element.13, f32[768]{0:T(1024)} %get-tuple-element.11, f32[768,10]{0,1:T(8,128)} %fusion.74), channel_id=1, replica_groups=mesh['dp'=4,'expert'=8] {'expert'}, use_global_device_ids=true, to_apply=%region_29.30 | all-reduce | flops 9216 | bytes 73728 | tf_op jit(solution)/shard_map/psum | solution.py:270
  507.7 21.6 %all-reduce.2 = (f32[768]{0:T(1024)}, f32[768]{0:T(1024)}, f32[768,10]{0,1:T(8,128)}) all-reduce(f32[768]{0:T(1024)} %get-tuple-element.25, f32[768]{0:T(1024)} %get-tuple-element.26, f32[768,10]{0,1:T(8,128)} %get-tuple-element.27), channel_id=1, replica_groups=mesh['dp'=4,'expert'=8] {'dp'}, use_global_device_ids=true, to_apply=%region_30.31 | all-reduce | flops 9216 | bytes 73728 | tf_op jit(solution)/shard_map/psum | solution.py:270
  539.5 310.7 %all-reduce.9.cloned.1.call-done = (f32[768,768]{1,0:T(8,128)}, f32[768,768]{1,0:T(8,128)}, f32[768,768]{1,0:T(8,128)}, f32[768,768]{1,0:T(8,128)}) async-done(((f32[768,768]{1,0:T(8,128)}, f32[768,768]{1,0:T(8,128)}, f32[768,768]{1,0:T(8,128)}, f32[768,768]{1,0:T(8,128)}), (f32[768,768]{1,0:T(8,128)}, f32[768,768]{1,0:T(8,128)}, f32[768,768]{1,0:T(8,128)}, ...) | async-done | bytes 9437200 | tf_op jit(solution)/shard_map/psum | solution.py:270
  (258 shorter events, 144.9 us)
Async XLA Ops:
  8.0 17.3 %copy-start = (bf16[768,768]{1,0:T(8,128)(2,1)S(1)}, bf16[768,768]{1,0:T(8,128)(2,1)}, u32[]{:S(2)}) copy-start(bf16[768,768]{1,0:T(8,128)(2,1)} %param.21) | copy-start | bytes 3538948
  12.1 13.2 %copy-start.48 = (f32[512]{0:T(512)}, f32[512]{0:T(512)S(1)}, u32[]{:S(2)}) copy-start(f32[512]{0:T(512)S(1)} %broadcast_multiply_fusion.5) | copy-start | bytes 6148
  13.6 11.7 %copy-start.53 = (f32[512]{0:T(512)}, f32[512]{0:T(512)S(1)}, u32[]{:S(2)}) copy-start(f32[512]{0:T(512)S(1)} %add_rsqrt_fusion.1) | copy-start | bytes 6148
  14.4 31.7 %copy-start.44 = (s32[512,1]{0,1:T(1,128)}, s32[512,1]{0,1:T(1,128)S(1)}, u32[]{:S(2)}) copy-start(s32[512,1]{0,1:T(1,128)S(1)} %get-tuple-element.50) | copy-start | bytes 6148
  14.4 32.7 %copy-start.43 = (s32[512,1]{0,1:T(1,128)}, s32[512,1]{0,1:T(1,128)S(1)}, u32[]{:S(2)}) copy-start(s32[512,1]{0,1:T(1,128)S(1)} %get-tuple-element.49) | copy-start | bytes 6148
  20.6 9.5 %copy-start.8 = (bf16[512,768]{0,1:T(8,128)(2,1)}, bf16[512,768]{0,1:T(8,128)(2,1)S(1)}, u32[]{:S(2)}) copy-start(bf16[512,768]{0,1:T(8,128)(2,1)S(1)} %copy.82) | copy-start | bytes 2359300
  42.6 6.1 copy-start.2
  43.0 10.8 %copy-start.41 = (f32[512]{0:T(512)}, f32[512]{0:T(512)S(1)}, u32[]{:S(2)}) copy-start(f32[512]{0:T(512)S(1)} %add_rsqrt_fusion) | copy-start | bytes 6148
  49.1 7.0 copy-start.60
  58.6 54.6 %all-to-all-start = ((bf16[8,102,768]{2,1,0:T(8,128)(2,1)}), bf16[8,102,768]{2,1,0:T(8,128)(2,1)}, u32[]{:S(2)}, u32[]{:S(2)}) async-start(bf16[8,102,768]{2,1,0:T(8,128)(2,1)} %broadcast_select_fusion), calls=%async_computation | async-start | bytes 2555904 | tf_op jit(solution)/shard_map/all_to_all | solution.py:152
  71.4 13.5 %copy-start.67 = (f32[512,2,3072]{2,0,1:T(8,128)}, f32[512,2,3072]{2,0,1:T(8,128)S(1)}, u32[]{:S(2)}) copy-start(f32[512,2,3072]{2,0,1:T(8,128)S(1)} %fusion.79) | copy-start | bytes 37748740
  71.4 13.5 %copy-start.16 = (bf16[512,768]{1,0:T(8,128)(2,1)S(1)}, bf16[512,768]{1,0:T(8,128)(2,1)}, u32[]{:S(2)}) copy-start(bf16[512,768]{1,0:T(8,128)(2,1)} %param.29) | copy-start | bytes 2359300
  84.9 6.1 copy-start.17
  113.3 50.3 %all-to-all-start.2 = ((bf16[8,102,768]{2,1,0:T(8,128)(2,1)}), bf16[8,102,768]{2,1,0:T(8,128)(2,1)}, u32[]{:S(2)}, u32[]{:S(2)}) async-start(bf16[8,102,768]{2,1,0:T(8,128)(2,1)} %multiply_convert_fusion.5), calls=%async_computation.2 | async-start | bytes 2555904 | tf_op jit(solution)/shard_map/all_to_all | solution.py:192
  134.8 11.8 %copy-start.68 = (f32[816,3072]{1,0:T(8,128)}, f32[816,3072]{1,0:T(8,128)S(1)}, u32[]{:S(2)}) copy-start(f32[816,3072]{1,0:T(8,128)S(1)} %fusion.26) | copy-start | bytes 30081028
  163.5 43.0 %all-to-all-start.1 = ((bf16[8,2,39168]{2,1,0:T(2,128)(2,1)}), bf16[8,2,39168]{2,1,0:T(2,128)(2,1)}, u32[]{:S(2)}, u32[]{:S(2)}) async-start(bf16[8,2,39168]{2,1,0:T(2,128)(2,1)} %reshape.542), calls=%async_computation.1 | async-start | bytes 2506752 | tf_op jit(solution)/shard_map/all_to_all | solution.py:156
  182.2 8.2 copy-start.66
  206.6 21.9 %all-to-all-start.3 = ((bf16[8,2,39168]{2,1,0:T(2,128)(2,1)}), bf16[8,2,39168]{2,1,0:T(2,128)(2,1)}, u32[]{:S(2)}, u32[]{:S(2)}) async-start(bf16[8,2,39168]{2,1,0:T(2,128)(2,1)} %reshape.544), calls=%async_computation.3 | async-start | bytes 2506752 | tf_op jit(solution)/shard_map/all_to_all | solution.py:198
  210.8 261.2 %all-reduce.7.cloned.1.call-start = ((), (), s32[]{:S(2)}) async-start(), calls=%async_computation.8 | async-start | bytes 18874368 | tf_op jit(solution)/shard_map/psum | solution.py:270
  252.0 12.9 %copy-start.42 = (f32[512]{0:T(512)S(1)}, f32[512]{0:T(512)}, u32[]{:S(2)}) copy-start(f32[512]{0:T(512)} %copy-done.41) | copy-start | bytes 6148
  261.4 24.9 %copy-start.52 = (f32[512]{0:T(512)}, f32[512]{0:T(512)S(1)}, u32[]{:S(2)}) copy-start(f32[512]{0:T(512)S(1)} %multiply_reduce_fusion.7) | copy-start | bytes 6148
  296.7 7.6 copy-start.15
  296.7 17.1 %slice-start = ((s8[12582912]{0:T(1024)(128)(4,1)}), s8[4194304]{0:T(1024)(128)(4,1)S(1)}, s32[]{:S(2)}) async-start(s8[12582912]{0:T(1024)(128)(4,1)} %bitcast.152), calls=%async_computation.10 | async-start | bytes 8388608
  296.7 17.1 %slice-start.1 = ((s8[12582912]{0:T(1024)(128)(4,1)}), s8[4194304]{0:T(1024)(128)(4,1)S(1)}, s32[]{:S(2)}) async-start(s8[12582912]{0:T(1024)(128)(4,1)} %bitcast.152), calls=%async_computation.11 | async-start | bytes 8388608
  304.2 9.5 %slice-start.2 = ((s8[12582912]{0:T(1024)(128)(4,1)}), s8[4194304]{0:T(1024)(128)(4,1)S(1)}, s32[]{:S(2)}) async-start(s8[12582912]{0:T(1024)(128)(4,1)} %bitcast.152), calls=%async_computation.12 | async-start | bytes 8388608
  313.8 7.1 copy-start.11
  324.1 5.4 copy-start.18
  331.9 201.9 %reduce-scatter.5.cloned.1.call-start = ((), (), s32[]{:S(2)}) async-start(), calls=%async_computation.7 | async-start | bytes 5898240 | tf_op jit(solution)/shard_map/reduce_scatter | solution.py:211
  344.4 192.2 %reduce-scatter.3.cloned.1.call-start = ((), (), s32[]{:S(2)}) async-start(), calls=%async_computation.6 | async-start | bytes 5898240 | tf_op jit(solution)/shard_map/reduce_scatter | solution.py:208
  355.1 495.1 %all-reduce.9.cloned.1.call-start = ((), (), s32[]{:S(2)}) async-start(), calls=%async_computation.9 | async-start | bytes 18874368 | tf_op jit(solution)/shard_map/psum | solution.py:270
  473.4 5.1 copy-start.65
  479.6 51.1 %copy-start.5 = (f32[512,768]{1,0:T(8,128)S(1)}, f32[512,768]{1,0:T(8,128)}, u32[]{:S(2)}) copy-start(f32[512,768]{1,0:T(8,128)} %copy-done.4) | copy-start | bytes 4718596
  (48 other events, 120.6 us)
Sparse Core Ops, SparseCore 0:
  332.0 139.9 all-reduce.6
Sparse Core Ops, SparseCore 1:
  344.5 86.1 reduce-scatter.4
  432.9 86.7 reduce-scatter.2
  522.6 327.5 all-reduce.8
